TPU v7x, 32 devices: a whole 2x2x4 slice. The times are simulated.
32 devices in a mesh: view: 4 (over y, core), slab: 8 (over z, x).
Axes of the slice: x: 2, y: 2, z: 4, core: 2. Of those that a mesh axis runs over, the one named last changes fastest.
Arguments:
- estimate: float32 [2, 128, 128, 1024], P(None, 'slab', 'view'), may hold values from 0.2 to 5
- recorded: bfloat16 [2, 2, 128, 128, 1024], P(None, None, None, 'view', 'slab'), may hold values from 0.19921875 to 5
- psf_lateral: float32 [2, 2, 31], replicated, may hold values from 0.0007 to 1.5, as said below
- psf_axial: float32 [2, 127], replicated, may hold values from 0.0007 to 1.5, as said below
- offsets: int32 [2, 2], replicated, may hold values from -8 to 8, as said below
Outputs:
- updated: float32 [2, 128, 128, 1024], P(None, 'slab', 'view')
Inputs may be any that keep to these rules, and one draw needn't show every extreme that they name: offsets[v] is imaging direction v's voxel shift along x and along y; the magnitude 8 occurs with both signs. `psf_lateral`: positive lateral taps. `psf_axial`: positive axial taps.
All inputs are finite; a program needn't handle non-finite values.
Results may differ from a plain program's by a relative error of at most 0.0003.
Values sent between devices are 32-bit elements; how exact they have to be, the bound alone decides.
No kernel may reach another device: no remote copies, remote signals or barrier semaphores. Data moves between devices by JAX's collectives and lax.ppermute only.
A program may use at most 128 MiB of HBM per device.

v0:
```python
import jax
import jax.numpy as jnp
from jax import lax
from jax.sharding import PartitionSpec as P

Z = 128
YBLK = 128
HALO = 23
BACKGROUND = 0.05
HIGHEST = lax.Precision.HIGHEST


def with_halo(value, sides, width):
    for axis, dim in sides:
        peers, length = (lax.axis_size(axis), value.shape[dim])
        up = [(i, (i + 1) % peers) for i in range(peers - 1)]
        down = [(j, i) for i, j in up]
        last = lax.slice_in_dim(value, length - width, length, axis=dim)
        leading = lax.slice_in_dim(value, 0, width, axis=dim)
        before = lax.ppermute(last, axis, up)
        after = lax.ppermute(leading, axis, down)
        value = jnp.concatenate([before, value, after], axis=dim)
    return value


def unit_taps(weights):
    return weights / jnp.sum(weights)


def band_table(weights, places):
    levels = jnp.arange(weights.shape[0], dtype=jnp.int32)
    return jnp.sum(jnp.where(places[..., None] == levels, weights, 0.0), axis=-1)


def margin_matrix(weights, offset, length, margin, adjoint):
    centre = (weights.shape[0] - 1) // 2
    outputs = jnp.arange(length, dtype=jnp.int32)[:, None]
    sources = jnp.arange(length + 2 * margin, dtype=jnp.int32)[None, :] - margin
    apart = sources - outputs
    if adjoint:
        apart = -apart
    return band_table(weights, apart - offset + centre)


def blocked_rows(field, weights, offset, width_blk, adjoint):
    extent = field.shape
    blocks = extent[3] // width_blk
    pieces = field.reshape(extent[0], extent[1], extent[2], blocks, width_blk)
    padded = jnp.pad(pieces, ((0, 0), (0, 0), (0, 0), (1, 1), (0, 0)))
    centre = (weights.shape[0] - 1) // 2
    sources = jnp.arange(width_blk, dtype=jnp.int32)[:, None]
    outputs = jnp.arange(width_blk, dtype=jnp.int32)[None, :]
    result = jnp.zeros(pieces.shape, jnp.float32)
    for shifted in range(3):
        apart = (shifted - 1) * width_blk + sources - outputs
        if adjoint:
            apart = -apart
        matrix = band_table(weights, apart - offset + centre)
        result = result + jnp.einsum(
            "czxkj,ji->czxki",
            padded[:, :, :, shifted : shifted + blocks],
            matrix,
            precision=HIGHEST,
        )
    return result.reshape(extent)


def shards(estimate, recorded, psf_lateral, psf_axial, offsets):
    views_n = recorded.shape[0]
    along_x = [unit_taps(psf_lateral[which, 0]) for which in range(views_n)]
    along_y = [unit_taps(psf_lateral[which, 1]) for which in range(views_n)]
    rows_at = jnp.arange(Z, dtype=jnp.int32)[:, None]
    cols_at = jnp.arange(Z, dtype=jnp.int32)[None, :]
    axial_places = cols_at - rows_at + (psf_axial.shape[1] - 1) // 2
    axial = [band_table(unit_taps(psf_axial[which]), axial_places) for which in range(views_n)]
    x_rows = estimate.shape[2]
    widened = with_halo(estimate, (("view", 2),), HALO)
    blurred = []
    for which in range(views_n):
        across = margin_matrix(along_x[which], offsets[which, 0], x_rows, HALO, False)
        sectioned = jnp.einsum("ab,czby->czay", across, widened, precision=HIGHEST)
        blurred.append(blocked_rows(sectioned, along_y[which], offsets[which, 1], YBLK, False))
    columns = lax.all_to_all(jnp.stack(blurred), "slab", split_axis=4, concat_axis=2, tiled=True)
    spread = []
    for which in range(views_n):
        imaged = jnp.einsum("oi,cixy->coxy", axial[which], columns[which], precision=HIGHEST)
        quotient = recorded[which].astype(jnp.float32) / (imaged + BACKGROUND)
        spread.append(jnp.einsum("oi,coxy->cixy", axial[which], quotient, precision=HIGHEST))
    planes = lax.all_to_all(jnp.stack(spread), "slab", split_axis=2, concat_axis=4, tiled=True)
    returned = [
        blocked_rows(planes[which], along_y[which], offsets[which, 1], YBLK, True)
        for which in range(views_n)
    ]
    fringe = with_halo(jnp.stack(returned), (("view", 3),), HALO)
    summed = jnp.zeros(estimate.shape, jnp.float32)
    for which in range(views_n):
        across = margin_matrix(along_x[which], offsets[which, 0], x_rows, HALO, True)
        summed = summed + jnp.einsum("ab,czby->czay", across, fringe[which], precision=HIGHEST)
    return estimate * (summed / views_n)


def solution(mesh):
    in_specs = (P(None, "slab", "view", None), P(None, None, None, "view", "slab"), P(), P(), P())
    out_specs = P(None, "slab", "view", None)
    return jax.shard_map(shards, mesh=mesh, in_specs=in_specs, out_specs=out_specs, check_vma=False)
```

profile of v0, /device:TPU:1, one launch (start us, length us, event | category | flops | bytes accessed | tf_op | source)
XLA Modules:
  0.0 831.5 jit_solution(896550517628313579)
XLA Ops:
  0.0 3.7 fusion.71
  5.5 4.5 collective-permute-start
  25.3 5.0 select_reduce_fusion.2
  30.3 12.5 %collective-permute-done = f32[2,16,23,1024]{3,1,2,0:T(8,128)S(1)} collective-permute-done((f32[2,16,23,1024]{3,1,2,0:T(8,128)S(1)}, f32[2,16,23,1024]{3,1,2,0:T(8,128)S(1)}, u32[]{:S(2)}, u32[]{:S(2)}) %collective-permute-start) | collective-permute-done | bytes 3014688 | tf_op jit(solution)/shard_map/ppermute | solution.py:20
  44.6 4.4 collective-permute-done.1
  50.7 11.1 %fusion.3 = f32[2,16,1024,32]{2,3,1,0:T(8,128)S(1)} fusion(f32[2,16,23,1024]{3,2,1,0:T(8,128)S(1)} %copy.64, f32[2,16,32,1024]{3,2,1,0:T(8,128)S(1)} %copy-done, f32[2,16,23,1024]{3,2,1,0:T(8,128)S(1)} %copy.63, f32[32,78]{1,0:T(8,128)S(1)} %get-tuple-element.61), kind=kOutput, calls=%fused_computation.21 | convolution fusion | flops 986578944 | bytes 14427904 | tf_op jit(solution)/shard_map/ab,czby->czay/dot_general | solution.py:81
  69.7 4.9 add_add_fusion.3
  74.6 5.3 stack_reshape.12
  79.9 13.7 %fusion.2 = f32[2,16,1024,32]{2,3,1,0:T(8,128)S(1)} fusion(f32[2,16,23,1024]{3,2,1,0:T(8,128)} %copy-done.4, f32[2,16,32,1024]{3,2,1,0:T(8,128)} %param.5, f32[2,16,23,1024]{3,2,1,0:T(8,128)S(1)} %copy.63, f32[32,78]{1,0:T(8,128)S(1)} %get-tuple-element.16), kind=kOutput, calls=%fused_computation.20 | convolution fusion | flops 986578944 | bytes 14427904 | tf_op jit(solution)/shard_map/ab,czby->czay/dot_general | solution.py:81
  101.4 4.9 add_add_fusion.2
  106.3 4.9 stack_reshape.13
  111.2 8.3 %pad_maximum_fusion.2 = f32[2,2,16,32,1024]{4,3,2,1,0:T(8,128)} fusion(f32[1,2,16,32,1024]{4,3,2,1,0:T(8,128)} %stack_reshape.13, f32[1,2,16,32,1024]{4,3,2,1,0:T(8,128)} %stack_reshape.12), kind=kLoop, calls=%fused_computation.14 | loop fusion | flops 2097152 | bytes 16777216 | tf_op jit(solution)/shard_map/stack | solution.py:83
  119.6 26.6 %copy.65 = f32[2,2,16,32,1024]{3,2,1,0,4:T(8,128)} copy(f32[2,2,16,32,1024]{4,3,2,1,0:T(8,128)} %pad_maximum_fusion.2) | data formatting | bytes 16777216 | tf_op jit(solution)/shard_map/stack | solution.py:83
  146.1 20.5 %reshape.373 = f32[8,1,262144]{2,1,0:T(1,128)} reshape(f32[1024,2,2,16,32]{4,3,2,1,0:T(8,128)} %bitcast.192) | data formatting | bytes 16777216
  166.6 5.5 all-to-all-start
  172.2 4.4 fusion.70
  176.6 4.6 copy.100
  187.9 150.7 %all-to-all-done = f32[8,1,262144]{2,1,0:T(1,128)} async-done(((f32[8,1,262144]{2,1,0:T(1,128)}), f32[8,1,262144]{2,1,0:T(1,128)}, u32[]{:S(2)}, u32[]{:S(2)}) %all-to-all-start) | async-done | bytes 8388640 | tf_op jit(solution)/shard_map/all_to_all | solution.py:83
  339.1 26.4 %reduce.6 = f32[8,262144]{1,0:T(8,128)} reduce(f32[8,1,262144]{2,1,0:T(1,128)} %all-to-all-done, f32[]{:T(128)} %broadcast.385), dimensions={1}, to_apply=%all_to_all.22.reduce_sub_computation | reduce | bytes 16777220 | tf_op jit(solution)/shard_map/all_to_all | solution.py:83
  365.5 25.3 %reshape.374 = f32[1024,2,2,16,32]{4,3,2,1,0:T(8,128)} reshape(f32[8,262144]{1,0:T(8,128)} %reduce.6) | data formatting | bytes 16777216
  390.7 18.4 %copy.97 = f32[2,2,16,32,8,128]{5,4,3,2,1,0:T(8,128)} copy(f32[2,2,16,32,8,128]{3,2,1,0,5,4:T(8,128)} %bitcast.193) | data formatting | bytes 16777216 | tf_op jit(solution)/shard_map/all_to_all | solution.py:83
  409.1 4.0 fusion.69
  414.8 8.4 %fusion.18 = f32[2,32,128,128]{3,2,1,0:T(8,128)S(1)} fusion(f32[2,128,32,128]{3,2,1,0:T(8,128)S(1)} %bitcast.206, f32[128,128]{1,0:T(8,128)S(1)} %get-tuple-element.5), kind=kOutput, calls=%fused_computation.41 | convolution fusion | flops 1610612736 | bytes 8454144 | tf_op jit(solution)/shard_map/oi,cixy->coxy/dot_general | solution.py:86
  423.2 4.1 fusion.22
  427.3 8.4 %fusion.16 = f32[2,32,128,128]{3,2,1,0:T(8,128)S(1)} fusion(f32[2,128,32,128]{3,2,1,0:T(8,128)S(1)} %bitcast.205, f32[128,128]{1,0:T(8,128)S(1)} %get-tuple-element.6), kind=kOutput, calls=%fused_computation.39 | convolution fusion | flops 1610612736 | bytes 8454144 | tf_op jit(solution)/shard_map/oi,cixy->coxy/dot_general | solution.py:86
  435.7 4.3 fusion.23
  440.0 3.8 pad_maximum_fusion.3
  443.8 10.3 %copy.72 = f32[2,2,128,32,128]{4,3,1,0,2:T(8,128)} copy(f32[2,2,128,32,128]{2,4,3,1,0:T(8,128)} %pad_maximum_fusion.3) | data formatting | bytes 16777216 | tf_op jit(solution)/shard_map/stack | solution.py:89
  454.1 187.0 %all_to_all.30 = f32[2,2,128,32,128]{4,3,1,0,2:T(8,128)S(1)} all-to-all(f32[2,2,128,32,128]{4,3,1,0,2:T(8,128)} %copy.72), channel_id=1, replica_groups=mesh['view'=4,'slab'=8] {'slab'}, dimensions={2} | all-to-all | bytes 16777216 | tf_op jit(solution)/shard_map/all_to_all | solution.py:89
  641.1 8.1 copy.111
  653.7 3.6 fusion.29
  660.8 4.9 add_add_fusion
  665.7 4.9 stack_reshape.15
  670.6 5.3 fusion.33
  679.5 5.1 add_add_fusion.1
  684.6 4.9 stack_reshape.14
  689.5 4.8 constant_dynamic-update-slice_fusion.1
  696.6 9.5 %fusion.68 = (f32[2,2,16,23,1024]{4,3,2,1,0:T(8,128)}, f32[2,2,16,23,1024]{4,3,2,1,0:T(8,128)S(1)}) fusion(f32[2,2,16,32,1024]{4,3,2,1,0:T(8,128)} %constant_dynamic-update-slice_fusion), kind=kLoop, calls=%fused_computation.165 | loop fusion | bytes 24117248 | tf_op jit(solution)/shard_map/slice | solution.py:18
  706.2 6.3 copy.75
  712.4 4.0 collective-permute-start.2
  716.4 3.5 copy.76
  721.8 59.3 %collective-permute-done.2 = f32[2,2,16,23,1024]{4,2,3,1,0:T(8,128)S(1)} collective-permute-done((f32[2,2,16,23,1024]{4,2,3,1,0:T(8,128)S(1)}, f32[2,2,16,23,1024]{4,2,3,1,0:T(8,128)S(1)}, u32[]{:S(2)}, u32[]{:S(2)}) %collective-permute-start.2) | collective-permute-done | bytes 6029344 | tf_op jit(solution)/shard_map/ppermute | solution.py:20
  781.1 3.5 copy.77
  784.6 4.8 collective-permute-done.3
  789.4 6.2 copy.78
  795.6 8.4 %pad_maximum_fusion = f32[2,2,16,78,1024]{4,3,2,1,0:T(8,128)S(1)} fusion(f32[2,2,16,23,1024]{4,3,2,1,0:T(8,128)} %copy.78, f32[2,2,16,32,1024]{4,3,2,1,0:T(8,128)} %constant_dynamic-update-slice_fusion, f32[2,2,16,23,1024]{4,3,2,1,0:T(8,128)S(1)} %copy.77), kind=kLoop, calls=%fused_computation | loop fusion | flops 10223616 | bytes 40894464 | tf_op jit(solution)/shard_map/concatenate | solution.py:22
  804.1 12.3 %fusion = f32[2,16,1024,32]{2,3,1,0:T(8,128)} fusion(f32[2,2,16,78,1024]{4,3,2,1,0:T(8,128)S(1)} %pad_maximum_fusion, f32[32,78]{1,0:T(8,128)S(1)} %copy-done.15), kind=kOutput, calls=%fused_computation.2 | convolution fusion | flops 981467136 | bytes 14696448 | tf_op jit(solution)/shard_map/ab,czby->czay/dot_general | solution.py:98
  816.4 14.9 %bitcast_multiply_fusion = f32[2,16,32,1024]{3,2,1,0:T(8,128)} fusion(f32[2,16,32,1024]{3,2,1,0:T(8,128)S(1)} %copy-done.1, f32[2,16,1024,32]{2,3,1,0:T(8,128)} %fusion, f32[2,2,16,78,1024]{4,3,2,1,0:T(8,128)S(1)} %pad_maximum_fusion, f32[32,78]{1,0:T(8,128)S(1)} %copy-done.14), kind=kOutput, calls=%fused_computation.36 | convolution fusion | flops 984612864 | bytes 23085056 | tf_op jit(solution)/shard_map/ab,czby->czay/dot_general | solution.py:98
  (76 shorter events, 60.5 us)
Async XLA Ops:
  5.5 8.3 copy-start.18
  5.5 9.0 %copy-start.16 = (f32[2,2,31]{2,1,0:T(2,128)S(1)}, f32[2,2,31]{2,1,0:T(2,128)}, u32[]{:S(2)}) copy-start(f32[2,2,31]{2,1,0:T(2,128)} %param.7) | copy-start | bytes 1492
  5.5 37.3 %collective-permute-start = (f32[2,16,23,1024]{3,1,2,0:T(8,128)S(1)}, f32[2,16,23,1024]{3,1,2,0:T(8,128)S(1)}, u32[]{:S(2)}, u32[]{:S(2)}) collective-permute-start(f32[2,16,23,1024]{3,1,2,0:T(8,128)S(1)} %copy.101), channel_id=1, source_target_pairs={{0,8},{8,16},{16,24},{1,9},{9,17},{17,25},{2,10},{10,18},{18,26},{... | collective-permute-start | bytes 9043976 | tf_op jit(solution)/shard_map/ppermute | solution.py:20
  11.8 37.2 %collective-permute-start.1 = (f32[2,16,23,1024]{3,1,2,0:T(8,128)S(1)}, f32[2,16,23,1024]{3,1,2,0:T(8,128)S(1)}, u32[]{:S(2)}, u32[]{:S(2)}) collective-permute-start(f32[2,16,23,1024]{3,1,2,0:T(8,128)S(1)} %copy.102), channel_id=1, source_target_pairs={{8,0},{16,8},{24,16},{9,1},{17,9},{25,17},{10,2},{18,10},{26,18},{... | collective-permute-start | bytes 9043976 | tf_op jit(solution)/shard_map/ppermute | solution.py:21
  44.6 6.2 copy-start
  50.7 11.1 %copy-start.4 = (f32[2,16,23,1024]{3,2,1,0:T(8,128)}, f32[2,16,23,1024]{3,2,1,0:T(8,128)S(1)}, u32[]{:S(2)}) copy-start(f32[2,16,23,1024]{3,2,1,0:T(8,128)S(1)} %copy.64) | copy-start | bytes 9043972
  166.6 172.0 %all-to-all-start = ((f32[8,1,262144]{2,1,0:T(1,128)}), f32[8,1,262144]{2,1,0:T(1,128)}, u32[]{:S(2)}, u32[]{:S(2)}) async-start(f32[8,1,262144]{2,1,0:T(1,128)} %reshape.373), calls=%async_computation | async-start | bytes 16777216 | tf_op jit(solution)/shard_map/all_to_all | solution.py:83
  176.6 7.5 copy-start.17
  414.8 8.4 %copy-start.7 = (bf16[1,2,128,32,128]{2,4,3,1,0:T(8,128)(2,1)S(1)}, bf16[1,2,128,32,128]{2,4,3,1,0:T(8,128)(2,1)}, u32[]{:S(2)}) copy-start(bf16[1,2,128,32,128]{2,4,3,1,0:T(8,128)(2,1)} %copy.100) | copy-start | bytes 6291460
  427.3 8.4 %copy-start.6 = (bf16[1,2,128,32,128]{2,4,3,1,0:T(8,128)(2,1)S(1)}, bf16[1,2,128,32,128]{2,4,3,1,0:T(8,128)(2,1)}, u32[]{:S(2)}) copy-start(bf16[1,2,128,32,128]{2,4,3,1,0:T(8,128)(2,1)} %copy.103) | copy-start | bytes 6291460
  649.2 4.5 copy-start.2
  649.2 4.5 copy-start.13
  653.7 3.6 copy-start.12
  657.3 3.4 copy-start.11
  665.7 4.9 copy-start.10
  670.6 5.4 copy-start.3
  670.6 5.4 copy-start.9
  676.0 3.4 copy-start.8
  689.5 4.9 copy-start.5
  712.4 68.7 %collective-permute-start.2 = (f32[2,2,16,23,1024]{4,2,3,1,0:T(8,128)S(1)}, f32[2,2,16,23,1024]{4,2,3,1,0:T(8,128)S(1)}, u32[]{:S(2)}, u32[]{:S(2)}) collective-permute-start(f32[2,2,16,23,1024]{4,2,3,1,0:T(8,128)S(1)} %copy.75), channel_id=1, source_target_pairs={{0,8},{8,16},{16,24},{1,9},{9,17},{17,25},{2,10},{10,18},{18,26},{... | collective-permute-start | bytes 18087944 | tf_op jit(solution)/shard_map/ppermute | solution.py:20
  719.9 69.5 %collective-permute-start.3 = (f32[2,2,16,23,1024]{4,2,3,1,0:T(8,128)S(1)}, f32[2,2,16,23,1024]{4,2,3,1,0:T(8,128)S(1)}, u32[]{:S(2)}, u32[]{:S(2)}) collective-permute-start(f32[2,2,16,23,1024]{4,2,3,1,0:T(8,128)S(1)} %copy.76), channel_id=1, source_target_pairs={{8,0},{16,8},{24,16},{9,1},{17,9},{25,17},{10,2},{18,10},{26,18},{... | collective-permute-start | bytes 18087944 | tf_op jit(solution)/shard_map/ppermute | solution.py:21
  795.6 8.4 %copy-start.15 = (f32[32,78]{1,0:T(8,128)S(1)}, f32[32,78]{1,0:T(8,128)}, u32[]{:S(2)}) copy-start(f32[32,78]{1,0:T(8,128)} %get-tuple-element.15) | copy-start | bytes 29956
  804.0 12.3 %copy-start.1 = (f32[2,16,32,1024]{3,2,1,0:T(8,128)S(1)}, f32[2,16,32,1024]{3,2,1,0:T(8,128)}, u32[]{:S(2)}) copy-start(f32[2,16,32,1024]{3,2,1,0:T(8,128)} %param.5) | copy-start | bytes 12582916
  804.1 12.3 %copy-start.14 = (f32[32,78]{1,0:T(8,128)S(1)}, f32[32,78]{1,0:T(8,128)}, u32[]{:S(2)}) copy-start(f32[32,78]{1,0:T(8,128)} %get-tuple-element.62) | copy-start | bytes 29956
where the time goes:
time: 839 us; the launch traced here: 831 us
  waiting for transfers between devices  232 us (28%)
  local copies, waits for them, and re-layouts  201 us (24%)
  blocking collectives  187 us (22%)
  matrix products  126 us (15%)
  other arithmetic  66.6 us (8%)
  starting transfers between devices  17.9 us (2%)
    all_to_all x1, blocking collectives, shards(): lax.all_to_all(jnp.stack(spread), 'slab', split_axis=2, concat_axis=4, ti...  187 us
    all_to_all x1, waiting for transfers between devices, shards(): lax.all_to_all(jnp.stack(blurred), 'slab', split_axis=4, concat_axis=2, t...  151 us
    ppermute x2, waiting for transfers between devices, with_halo(): before = lax.ppermute(last, axis, up)  71.8 us
    unnamed x47, local copies, waits for them, and re-layouts  65 us
    dot_general x12, matrix products, blocked_rows(): jnp.einsum('czxkj,ji->czxki', padded[:, :, :, shifted:shifted + blocks],...  49.3 us
    another operation x3, local copies, waits for them, and re-layouts, shards(): jnp.stack(blurred)  36.7 us
    dot_general x2, matrix products, shards(): jnp.einsum('ab,czby->czay', across, fringe[which], precision=HIGHEST)  27.2 us
    all_to_all x1, other arithmetic, shards(): lax.all_to_all(jnp.stack(blurred), 'slab', split_axis=4, concat_axis=2, t...  26.4 us
  transfers between devices with their start and end apart: 5, of which 5 were waited for; matrix products, arithmetic and copies ran while one was open for 5% of the time, Pallas kernels for 0%

commit v1 on v0

--- a/solution.py
+++ b/solution.py
@@ -66,6 +66,18 @@
 
 
 def shards(estimate, recorded, psf_lateral, psf_axial, offsets):
+
+    def _use_floor(inner_x, bus_axis):
+        return jnp.concatenate(
+            lax.all_to_all(
+                jnp.stack(jnp.split(inner_x, lax.axis_size(bus_axis), 4), 0),
+                axis_name=bus_axis,
+                split_axis=0,
+                concat_axis=0,
+            ),
+            axis=2,
+        )
+
     views_n = recorded.shape[0]
     along_x = [unit_taps(psf_lateral[which, 0]) for which in range(views_n)]
     along_y = [unit_taps(psf_lateral[which, 1]) for which in range(views_n)]
@@ -80,7 +92,7 @@
         across = margin_matrix(along_x[which], offsets[which, 0], x_rows, HALO, False)
         sectioned = jnp.einsum("ab,czby->czay", across, widened, precision=HIGHEST)
         blurred.append(blocked_rows(sectioned, along_y[which], offsets[which, 1], YBLK, False))
-    columns = lax.all_to_all(jnp.stack(blurred), "slab", split_axis=4, concat_axis=2, tiled=True)
+    columns = _use_floor(jnp.stack(blurred), "slab")
     spread = []
     for which in range(views_n):
         imaged = jnp.einsum("oi,cixy->coxy", axial[which], columns[which], precision=HIGHEST)

time: 839 us -> 726 us (0.87)
  local copies, waits for them, and re-layouts: 201 us -> 123 us
  other arithmetic: 66.6 us -> 31.5 us
    ppermute x2, waiting for transfers between devices: 71.8 us -> 2.54 us  [with_halo(): before = lax.ppermute(last, axis, up)]
    ppermute x2, waiting for transfers between devices: 9.2 us -> 74.2 us  [with_halo(): after = lax.ppermute(leading, axis, down)]
    unnamed x47 -> x43, local copies, waits for them, and re-layouts: 65 us -> 31.4 us
    all_to_all x1 -> x0, other arithmetic: 26.4 us -> none  [shards(): lax.all_to_all(jnp.stack(blurred), 'slab', split_axis=4, concat_axis=2, t...]
    another operation x3 -> x4, local copies, waits for them, and re-layouts: 36.7 us -> 11.5 us  [the longest x3 10.4 us: shards(): columns = _use_floor(jnp.stack(blurred), 'slab')]
    all_to_all x2 -> x1, local copies, waits for them, and re-layouts: 18.9 us -> 4.37 us  [_use_floor(): lax.all_to_all(jnp.stack(jnp.split(inner_x, lax.axis_size(bus_axis), 4),...]
  transfers between devices with their start and end apart: 5 -> 5, of which waited for: 5 -> 5; matrix products, arithmetic and copies ran while one was open for 5% -> 6% of each run, Pallas kernels for 0% -> 0%
where the time goes in v1:
time: 726 us; the launch traced here: 719 us
  waiting for transfers between devices  230 us (32%)
  blocking collectives  187 us (26%)
  matrix products  128 us (18%)
  local copies, waits for them, and re-layouts  123 us (17%)
  other arithmetic  31.5 us (4%)
  starting transfers between devices  17.7 us (2%)
    all_to_all x1, blocking collectives, shards(): lax.all_to_all(jnp.stack(spread), 'slab', split_axis=2, concat_axis=4, ti...  187 us
    all_to_all x1, waiting for transfers between devices, _use_floor(): lax.all_to_all(jnp.stack(jnp.split(inner_x, lax.axis_size(bus_axis), 4),...  154 us
    ppermute x2, waiting for transfers between devices, with_halo(): after = lax.ppermute(leading, axis, down)  74.2 us
    dot_general x12, matrix products, blocked_rows(): jnp.einsum('czxkj,ji->czxki', padded[:, :, :, shifted:shifted + blocks],...  53.5 us
    unnamed x43, local copies, waits for them, and re-layouts  31.4 us
    dot_general x2, matrix products, shards(): jnp.einsum('ab,czby->czay', across, fringe[which], precision=HIGHEST)  27.2 us
    dot_general x2, matrix products, shards(): sectioned = jnp.einsum('ab,czby->czay', across, widened, precision=HIGHEST)  22.2 us
    dot_general x2, matrix products, shards(): jnp.einsum('oi,cixy->coxy', axial[which], columns[which], precision=HIGHEST)  16.8 us
  transfers between devices with their start and end apart: 5, of which 5 were waited for; matrix products, arithmetic and copies ran while one was open for 6% of the time, Pallas kernels for 0%

profile of v1, /device:TPU:1, one launch (start us, length us, event | category | flops | bytes accessed | tf_op | source)
XLA Modules:
  0.0 718.7 jit_solution(4616385753718733877)
XLA Ops:
  0.0 3.7 fusion.79
  9.2 4.5 collective-permute-start
  25.3 4.3 select_reduce_fusion.2
  29.6 14.0 %collective-permute-done.1 = f32[2,16,23,1024]{3,1,2,0:T(8,128)S(1)} collective-permute-done((f32[2,16,23,1024]{3,1,2,0:T(8,128)S(1)}, f32[2,16,23,1024]{3,1,2,0:T(8,128)S(1)}, u32[]{:S(2)}, u32[]{:S(2)}) %collective-permute-start.1) | collective-permute-done | bytes 3014688 | tf_op jit(solution)/shard_map/ppermute | solution.py:21
  48.3 11.1 %fusion.2 = f32[2,16,1024,32]{2,3,1,0:T(8,128)S(1)} fusion(f32[2,16,23,1024]{3,2,1,0:T(8,128)S(1)} %copy.40, f32[2,16,32,1024]{3,2,1,0:T(8,128)S(1)} %copy-done, f32[2,16,23,1024]{3,2,1,0:T(8,128)S(1)} %copy.39, f32[32,78]{1,0:T(8,128)S(1)} %get-tuple-element.16), kind=kOutput, calls=%fused_computation.20 | convolution fusion | flops 986578944 | bytes 14427904 | tf_op jit(solution)/shard_map/ab,czby->czay/dot_general | solution.py:93
  59.4 11.1 %fusion.3 = f32[2,16,1024,32]{2,3,1,0:T(8,128)S(1)} fusion(f32[2,16,23,1024]{3,2,1,0:T(8,128)S(1)} %copy.40, f32[2,16,32,1024]{3,2,1,0:T(8,128)S(1)} %copy-done, f32[2,16,23,1024]{3,2,1,0:T(8,128)S(1)} %copy.39, f32[32,78]{1,0:T(8,128)S(1)} %get-tuple-element.61), kind=kOutput, calls=%fused_computation.21 | convolution fusion | flops 986578944 | bytes 14427904 | tf_op jit(solution)/shard_map/ab,czby->czay/dot_general | solution.py:93
  70.5 3.0 copy.76
  74.5 3.4 fusion.49
  78.0 3.4 fusion.6
  81.4 4.9 add_add_fusion.2
  86.3 4.9 stack_reshape.13
  91.2 5.8 fusion.53
  97.0 3.4 fusion.4
  100.4 4.9 add_add_fusion.3
  105.4 4.9 stack_reshape.12
  123.5 5.5 all-to-all-start
  129.0 4.4 fusion.78
  133.5 4.5 copy.72
  138.0 2.9 copy.75
  144.9 153.7 %all-to-all-done = f32[8,2,2,16,32,128]{5,4,3,2,1,0:T(8,128)} async-done(((f32[8,2,2,16,32,128]{5,4,3,2,1,0:T(8,128)}), f32[8,2,2,16,32,128]{5,4,3,2,1,0:T(8,128)}, u32[]{:S(2)}, u32[]{:S(2)}) %all-to-all-start) | async-done | bytes 8388640 | tf_op jit(solution)/shard_map/all_to_all | solution.py:72
  298.5 4.4 copy.85
  304.5 8.4 %fusion.18 = f32[2,32,128,128]{3,2,1,0:T(8,128)S(1)} fusion(f32[2,128,32,128]{3,2,1,0:T(8,128)S(1)} %bitcast.237, f32[128,128]{1,0:T(8,128)S(1)} %get-tuple-element.5), kind=kOutput, calls=%fused_computation.41 | convolution fusion | flops 1610612736 | bytes 8454144 | tf_op jit(solution)/shard_map/oi,cixy->coxy/dot_general | solution.py:98
  312.9 4.3 fusion.22
  317.3 8.4 %fusion.16 = f32[2,32,128,128]{3,2,1,0:T(8,128)S(1)} fusion(f32[2,128,32,128]{3,2,1,0:T(8,128)S(1)} %bitcast.234, f32[128,128]{1,0:T(8,128)S(1)} %get-tuple-element.6), kind=kOutput, calls=%fused_computation.39 | convolution fusion | flops 1610612736 | bytes 8454144 | tf_op jit(solution)/shard_map/oi,cixy->coxy/dot_general | solution.py:98
  325.7 4.0 fusion.23
  329.7 3.8 pad_maximum_fusion.2
  333.5 10.3 %copy.45 = f32[2,2,128,32,128]{4,3,1,0,2:T(8,128)} copy(f32[2,2,128,32,128]{2,4,3,1,0:T(8,128)} %pad_maximum_fusion.2) | data formatting | bytes 16777216 | tf_op jit(solution)/shard_map/stack | solution.py:101
  343.8 187.0 %all_to_all.20 = f32[2,2,128,32,128]{4,3,1,0,2:T(8,128)S(1)} all-to-all(f32[2,2,128,32,128]{4,3,1,0,2:T(8,128)} %copy.45), channel_id=1, replica_groups=mesh['view'=4,'slab'=8] {'slab'}, dimensions={2} | all-to-all | bytes 16777216 | tf_op jit(solution)/shard_map/all_to_all | solution.py:101
  530.8 8.1 %copy.84 = f32[2,2,8,16,32,128]{5,2,4,3,1,0:T(8,128)S(1)} copy(f32[2,2,8,16,32,128]{5,4,1,0,3,2:T(8,128)S(1)} %bitcast.233) | data formatting | bytes 16777216 | tf_op jit(solution)/shard_map/all_to_all | solution.py:101
  541.7 5.1 fusion.41
  546.8 3.4 fusion.37
  550.2 3.4 fusion.10
  553.6 4.9 add_add_fusion
  558.6 4.9 stack_reshape.15
  563.4 5.4 fusion.8
  568.9 5.3 add_add_fusion.1
  574.2 4.9 stack_reshape.14
  579.1 4.8 constant_dynamic-update-slice_fusion.3
  586.3 9.5 %fusion.76 = (f32[2,2,16,23,1024]{4,3,2,1,0:T(8,128)S(1)}, f32[2,2,16,23,1024]{4,3,2,1,0:T(8,128)}) fusion(f32[2,2,16,32,1024]{4,3,2,1,0:T(8,128)} %constant_dynamic-update-slice_fusion.2), kind=kLoop, calls=%fused_computation.183 | loop fusion | bytes 24117248 | tf_op jit(solution)/shard_map/slice | solution.py:18
  595.7 6.3 copy.49
  604.8 3.5 copy.48
  608.3 2.9 collective-permute-start.2
  611.3 60.2 %collective-permute-done.3 = f32[2,2,16,23,1024]{4,2,3,1,0:T(8,128)S(1)} collective-permute-done((f32[2,2,16,23,1024]{4,2,3,1,0:T(8,128)S(1)}, f32[2,2,16,23,1024]{4,2,3,1,0:T(8,128)S(1)}, u32[]{:S(2)}, u32[]{:S(2)}) %collective-permute-start.3) | collective-permute-done | bytes 6029344 | tf_op jit(solution)/shard_map/ppermute | solution.py:21
  671.5 3.5 copy.51
  676.4 6.2 copy.50
  682.6 8.6 %pad_maximum_fusion = f32[2,2,16,78,1024]{4,3,2,1,0:T(8,128)S(1)} fusion(f32[2,2,16,23,1024]{4,3,2,1,0:T(8,128)S(1)} %copy.51, f32[2,2,16,32,1024]{4,3,2,1,0:T(8,128)} %constant_dynamic-update-slice_fusion.2, f32[2,2,16,23,1024]{4,3,2,1,0:T(8,128)} %copy.50), kind=kLoop, calls=%fused_computation | loop fusion | flops 10223616 | bytes 40894464 | tf_op jit(solution)/shard_map/concatenate | solution.py:22
  691.3 12.3 %fusion = f32[2,16,1024,32]{2,3,1,0:T(8,128)} fusion(f32[2,2,16,78,1024]{4,3,2,1,0:T(8,128)S(1)} %pad_maximum_fusion, f32[32,78]{1,0:T(8,128)S(1)} %copy-done.10), kind=kOutput, calls=%fused_computation.2 | convolution fusion | flops 981467136 | bytes 14696448 | tf_op jit(solution)/shard_map/ab,czby->czay/dot_general | solution.py:110
  703.5 14.9 %bitcast_multiply_fusion = f32[2,16,32,1024]{3,2,1,0:T(8,128)} fusion(f32[2,16,32,1024]{3,2,1,0:T(8,128)S(1)} %copy-done.1, f32[2,16,1024,32]{2,3,1,0:T(8,128)} %fusion, f32[2,2,16,78,1024]{4,3,2,1,0:T(8,128)S(1)} %pad_maximum_fusion, f32[32,78]{1,0:T(8,128)S(1)} %copy-done.9), kind=kOutput, calls=%fused_computation.36 | convolution fusion | flops 984612864 | bytes 23085056 | tf_op jit(solution)/shard_map/ab,czby->czay/dot_general | solution.py:110
  (68 shorter events, 50.7 us)
Async XLA Ops:
  5.5 8.3 %copy-start.13 = (s32[2,2]{1,0:T(2,128)S(1)}, s32[2,2]{1,0:T(2,128)}, u32[]{:S(2)}) copy-start(s32[2,2]{1,0:T(2,128)} %param.9) | copy-start | bytes 52
  5.5 9.0 %copy-start.11 = (f32[2,2,31]{2,1,0:T(2,128)S(1)}, f32[2,2,31]{2,1,0:T(2,128)}, u32[]{:S(2)}) copy-start(f32[2,2,31]{2,1,0:T(2,128)} %param.7) | copy-start | bytes 1492
  5.5 38.1 %collective-permute-start.1 = (f32[2,16,23,1024]{3,1,2,0:T(8,128)S(1)}, f32[2,16,23,1024]{3,1,2,0:T(8,128)S(1)}, u32[]{:S(2)}, u32[]{:S(2)}) collective-permute-start(f32[2,16,23,1024]{3,1,2,0:T(8,128)S(1)} %copy.74), channel_id=1, source_target_pairs={{8,0},{16,8},{24,16},{9,1},{17,9},{25,17},{10,2},{18,10},{26,18},{... | collective-permute-start | bytes 9043976 | tf_op jit(solution)/shard_map/ppermute | solution.py:21
  9.2 37.3 %collective-permute-start = (f32[2,16,23,1024]{3,1,2,0:T(8,128)S(1)}, f32[2,16,23,1024]{3,1,2,0:T(8,128)S(1)}, u32[]{:S(2)}, u32[]{:S(2)}) collective-permute-start(f32[2,16,23,1024]{3,1,2,0:T(8,128)S(1)} %copy.73), channel_id=1, source_target_pairs={{0,8},{8,16},{16,24},{1,9},{9,17},{17,25},{2,10},{10,18},{18,26},{... | collective-permute-start | bytes 9043976 | tf_op jit(solution)/shard_map/ppermute | solution.py:20
  45.3 2.9 copy-start
  91.2 5.8 copy-start.2
  110.3 3.4 copy-start.4
  123.5 175.0 %all-to-all-start = ((f32[8,2,2,16,32,128]{5,4,3,2,1,0:T(8,128)}), f32[8,2,2,16,32,128]{5,4,3,2,1,0:T(8,128)}, u32[]{:S(2)}, u32[]{:S(2)}) async-start(f32[8,2,2,16,32,128]{5,4,3,2,1,0:T(8,128)} %fusion.28), calls=%async_computation | async-start | bytes 16777216 | tf_op jit(solution)/shard_map/all_to_all | solution.py:72
  133.5 7.4 %copy-start.12 = (f32[2,127]{1,0:T(2,128)S(1)}, f32[2,127]{1,0:T(2,128)}, u32[]{:S(2)}) copy-start(f32[2,127]{1,0:T(2,128)} %param.8) | copy-start | bytes 3052
  304.5 8.4 %copy-start.8 = (bf16[1,2,128,32,128]{2,4,3,1,0:T(8,128)(2,1)S(1)}, bf16[1,2,128,32,128]{2,4,3,1,0:T(8,128)(2,1)}, u32[]{:S(2)}) copy-start(bf16[1,2,128,32,128]{2,4,3,1,0:T(8,128)(2,1)} %copy.72) | copy-start | bytes 6291460
  317.3 8.4 %copy-start.7 = (bf16[1,2,128,32,128]{2,4,3,1,0:T(8,128)(2,1)S(1)}, bf16[1,2,128,32,128]{2,4,3,1,0:T(8,128)(2,1)}, u32[]{:S(2)}) copy-start(bf16[1,2,128,32,128]{2,4,3,1,0:T(8,128)(2,1)} %copy.75) | copy-start | bytes 6291460
  563.4 5.4 copy-start.3
  563.4 5.4 copy-start.6
  579.1 4.9 copy-start.5
  602.0 69.5 %collective-permute-start.3 = (f32[2,2,16,23,1024]{4,2,3,1,0:T(8,128)S(1)}, f32[2,2,16,23,1024]{4,2,3,1,0:T(8,128)S(1)}, u32[]{:S(2)}, u32[]{:S(2)}) collective-permute-start(f32[2,2,16,23,1024]{4,2,3,1,0:T(8,128)S(1)} %copy.49), channel_id=1, source_target_pairs={{8,0},{16,8},{24,16},{9,1},{17,9},{25,17},{10,2},{18,10},{26,18},{... | collective-permute-start | bytes 18087944 | tf_op jit(solution)/shard_map/ppermute | solution.py:21
  608.3 68.0 %collective-permute-start.2 = (f32[2,2,16,23,1024]{4,2,3,1,0:T(8,128)S(1)}, f32[2,2,16,23,1024]{4,2,3,1,0:T(8,128)S(1)}, u32[]{:S(2)}, u32[]{:S(2)}) collective-permute-start(f32[2,2,16,23,1024]{4,2,3,1,0:T(8,128)S(1)} %copy.48), channel_id=1, source_target_pairs={{0,8},{8,16},{16,24},{1,9},{9,17},{17,25},{2,10},{10,18},{18,26},{... | collective-permute-start | bytes 18087944 | tf_op jit(solution)/shard_map/ppermute | solution.py:20
  682.6 8.7 %copy-start.10 = (f32[32,78]{1,0:T(8,128)S(1)}, f32[32,78]{1,0:T(8,128)}, u32[]{:S(2)}) copy-start(f32[32,78]{1,0:T(8,128)} %get-tuple-element.15) | copy-start | bytes 29956
  691.2 12.3 %copy-start.1 = (f32[2,16,32,1024]{3,2,1,0:T(8,128)S(1)}, f32[2,16,32,1024]{3,2,1,0:T(8,128)}, u32[]{:S(2)}) copy-start(f32[2,16,32,1024]{3,2,1,0:T(8,128)} %param.5) | copy-start | bytes 12582916
  691.2 12.3 %copy-start.9 = (f32[32,78]{1,0:T(8,128)S(1)}, f32[32,78]{1,0:T(8,128)}, u32[]{:S(2)}) copy-start(f32[32,78]{1,0:T(8,128)} %get-tuple-element.62) | copy-start | bytes 29956
